TPU v7x, 256 devices: a whole 4x4x8 slice. The times are simulated.
256 devices in a mesh: tile: 64 (over y, x_hi, z), rcpt: 4 (over x_lo, core).
Axes of the slice: x: 4 (x_hi: 2, x_lo: 2; x = x_hi * 2 + x_lo), y: 4, z: 8, core: 2. Of those that a mesh axis runs over, the one named last changes fastest.
Arguments:
- adjoint_state: float32 [64, 16, 1024, 256], P('rcpt', None, 'tile'), may hold values from -6 to 6
- met_fields: bfloat16 [12, 3, 16, 1024, 256], P(None, None, 'rcpt', 'tile'), may hold values from -0.34960938 to 0.34960938
- forcing: bfloat16 [64, 1024, 256], P(None, 'tile'), may hold values from -6 to 6
- cluster_ids: int32 [64], P('rcpt'), may hold values from 0 to 63
- hour_index: int32 [2], replicated, may hold values from 0 to 11
Outputs:
- adjoint_out: float32 [64, 16, 1024, 256], P('rcpt', None, 'tile')
All inputs are finite; a program needn't handle non-finite values.
Results may differ from a plain program's by a relative error of at most 0.00035.
Values may be sent and summed in bfloat16 or wider, within the bound.
No kernel may reach another device: no remote copies, remote signals or barrier semaphores. Data moves between devices by JAX's collectives and lax.ppermute only.
A program may use at most 64 MiB of HBM per device.

v0:
```python
import jax
import jax.numpy as jnp
from jax import lax
from jax.sharding import PartitionSpec as P

STEPS = 2


def for_sending(x):

    def short(part):
        return part.astype(jnp.bfloat16) if part.dtype == jnp.float32 else part

    return jax.tree.map(short, x)


def passed_along(block, axis, distance):
    devices = range(lax.axis_size(axis))
    route = [((i - distance) % len(devices), i) for i in devices]
    return lax.ppermute(block, axis, route)


def interior(lam, winds, east, west):
    cx = winds[0].astype(jnp.float32)
    cy = winds[1].astype(jnp.float32)
    py = lam * jnp.maximum(cy, 0.0)
    my = lam * jnp.minimum(cy, 0.0)
    zero = jnp.zeros_like(py[..., :1])
    north = jnp.concatenate([py[..., 1:], zero], axis=3)
    south = jnp.concatenate([zero, my[..., :-1]], axis=3)
    return lam * (1.0 - jnp.abs(cx) - jnp.abs(cy)) + east - west + north - south


def horizontal_shift(lam, winds):
    cx = winds[0].astype(jnp.float32)
    px = lam * jnp.maximum(cx, 0.0)
    mx = lam * jnp.minimum(cx, 0.0)
    east_edge = passed_along(for_sending(px[:, :, :1]), "tile", -1)
    west_edge = passed_along(for_sending(mx[:, :, -1:]), "tile", 1)
    east = jnp.concatenate([px[:, :, 1:], east_edge], axis=2)
    west = jnp.concatenate([west_edge, mx[:, :, :-1]], axis=2)
    return interior(lam, winds, east, west)


def vertical(lam, mixing):
    coeff = 0.02 + 0.25 * jnp.abs(mixing.astype(jnp.float32))
    flux = coeff[:-1] * (lam[:, 1:] - lam[:, :-1])
    zero = jnp.zeros_like(flux[:, :1])
    return jnp.concatenate([flux, zero], axis=1) - jnp.concatenate([zero, flux], axis=1)


def finish(lam, flat, mixing, source_rows):
    state = flat + vertical(lam, mixing)
    return state.at[:, -1].add(source_rows)


def per_device(adjoint_state, met_fields, forcing, cluster_ids, hour_index):
    lam = adjoint_state
    clusters = forcing.shape[0]
    onehot = (cluster_ids[:, None] == jnp.arange(clusters, dtype=jnp.int32)[None, :]).astype(
        jnp.bfloat16
    )
    source_rows = jnp.dot(onehot, forcing.reshape(clusters, -1), preferred_element_type=jnp.float32)
    source_rows = source_rows.reshape(lam.shape[0], lam.shape[2], lam.shape[3])
    locals_list = [
        lax.dynamic_index_in_dim(met_fields, hour_index[step], 0, keepdims=False)
        for step in range(STEPS)
    ]
    for step in range(STEPS):
        metnow = lax.all_gather(locals_list[step], "rcpt", axis=1, tiled=True)
        lam_next = finish(lam, horizontal_shift(lam, metnow), metnow[2], source_rows)
        lam = lam_next
    return lam


def solution(mesh):
    placed = (
        P("rcpt", None, "tile", None),
        P(None, None, "rcpt", "tile", None),
        P(None, "tile", None),
        P("rcpt"),
        P(),
    )
    return jax.shard_map(
        per_device,
        mesh=mesh,
        in_specs=placed,
        out_specs=P("rcpt", None, "tile", None),
        check_vma=False,
    )
```

profile of v0, /device:TPU:1, one launch (start us, length us, event | category | flops | bytes accessed | tf_op | source)
XLA Modules:
  0.0 97.3 jit_solution(4686769854852998408)
XLA Ops:
  0.0 1.3 %fusion.32 = (s32[1]{0:T(128)}, s32[1]{0:T(128)}) fusion(s32[2]{0:T(128)} %param.13), kind=kLoop, calls=%fused_computation.69 | loop fusion | bytes 16 | tf_op jit(solution)/shard_map/slice | solution.py:66
  4.9 1.0 constant_dynamic-slice_fusion
  5.9 9.2 %all-gather = bf16[1,3,16,16,256]{4,3,2,1,0:T(8,128)(2,1)S(1)} all-gather(bf16[1,3,4,16,256]{4,3,2,1,0:T(8,128)(2,1)S(1)} %get-tuple-element.39), channel_id=2, replica_groups=mesh['tile'=64,'rcpt'=4] {'rcpt'}, dimensions={2}, use_global_device_ids=true | all-gather | bytes 491520 | tf_op jit(solution)/shard_map/all_gather | solution.py:70
  15.3 6.5 %fusion.31 = (f32[16,16,16,256]{3,0,2,1:T(8,128)S(1)}, f32[16,16,16,256]{3,0,2,1:T(8,128)S(1)}, f32[16,16,16,256]{3,0,2,1:T(8,128)S(1)}) fusion(f32[16,16,16,256]{3,2,1,0:T(8,128)} %param.9, f32[16,16,256]{2,1,0:T(8,128)S(1)} %get-tuple-element.47, f32[16,16,256]{2,1,0:T(8,128)S(1)} %get-tuple-element.50), kind=kLoop, calls=%fused_computation.68 | loop fusion | flops 2097152 | bytes 17301504 | tf_op args[0]
  23.4 8.6 %collective-permute-start = (bf16[16,16,1,256]{3,0,2,1:T(8,128)(2,1)}, bf16[16,16,1,256]{3,0,2,1:T(8,128)(2,1)}, u32[]{:S(2)}, u32[]{:S(2)}) collective-permute-start(bf16[16,16,1,256]{3,0,2,1:T(8,128)(2,1)} %slice.251), channel_id=1, source_target_pairs={{4,0},{8,4},{12,8},{16,12},{20,16},{24,20},{28,24},{32,28},{36,32}... | collective-permute-start | bytes 393224 | tf_op jit(solution)/shard_map/ppermute | solution.py:20
  32.0 2.3 %slice.182 = f32[16,16,15,256]{3,0,2,1:T(8,128)} slice(f32[16,16,16,256]{3,0,2,1:T(8,128)S(1)} %get-tuple-element.36), slice={[0:16], [0:16], [1:16], [0:256]} | slice | bytes 7864320 | tf_op jit(solution)/shard_map/slice | solution.py:40
  34.3 2.3 %slice.185 = f32[16,16,15,256]{3,0,2,1:T(8,128)} slice(f32[16,16,16,256]{3,0,2,1:T(8,128)S(1)} %get-tuple-element.37), slice={[0:16], [0:16], [0:15], [0:256]} | slice | bytes 7864320 | tf_op jit(solution)/shard_map/slice | solution.py:41
  36.6 6.7 %all-gather.1 = bf16[1,3,16,16,256]{4,3,2,1,0:T(8,128)(2,1)S(1)} all-gather(bf16[1,3,4,16,256]{4,3,2,1,0:T(8,128)(2,1)S(1)} %get-tuple-element.38), channel_id=3, replica_groups=mesh['tile'=64,'rcpt'=4] {'rcpt'}, dimensions={2}, use_global_device_ids=true | all-gather | bytes 491520 | tf_op jit(solution)/shard_map/all_gather | solution.py:70
  44.2 1.0 fusion.22
  46.1 2.5 %fusion.9 = f32[16,15,16,256]{3,0,2,1:T(8,128)} fusion(f32[16,16,16,256]{3,0,2,1:T(8,128)S(1)} %get-tuple-element.35, f32[15,16,256]{2,1,0:T(8,128)S(1)} %slice_bitcast_fusion.1), kind=kLoop, calls=%fused_computation.17 | loop fusion | flops 1966080 | bytes 12042240 | tf_op jit(solution)/shard_map/mul | solution.py:47
  48.6 3.0 %slice_multiply_fusion.3 = (f32[16,16,16,255]{3,0,2,1:T(8,128)S(1)}, f32[16,16,16,255]{3,0,2,1:T(8,128)S(1)}) fusion(f32[16,16,16,256]{3,0,2,1:T(8,128)S(1)} %get-tuple-element.35, f32[16,16,255]{2,1,0:T(8,128)} %slice.187, f32[16,16,255]{2,1,0:T(8,128)S(1)} %bitcast.53), kind=kLoop, calls=%fused_computation.3 | loop fusion | flops 2088960 | bytes 17233920 | tf_op jit(solution)/shard_map/mul | solution.py:26
  51.6 1.7 %slice_bitcast_fusion = f32[15,16,256]{2,1,0:T(8,128)} fusion(f32[1,16,16,256]{3,2,1,0:T(8,128)} %get-tuple-element.45), kind=kLoop, calls=%fused_computation.61 | loop fusion | bytes 491520 | tf_op jit(solution)/shard_map/slice | solution.py:47
  54.2 0.9 convert_element_type.53
  55.2 12.0 %fusion.3 = f32[16,16,16,256]{3,0,2,1:T(8,128)S(1)} fusion(f32[16,16,1,256]{3,0,2,1:T(8,128)S(1)} %convert_element_type.53, f32[16,16,15,256]{3,0,2,1:T(8,128)} %slice.182, f32[16,16,15,256]{3,0,2,1:T(8,128)} %slice.185, f32[16,16,1,256]{3,0,2,1:T(8,128)S(1)} %convert_element_type.54, f32[16,15,16,256]{3,0,2,1:T(8,128)} %fusion.9, ...), kind=kLoop, calls=%fused_computation.8 | loop fusion | flops 9437184 | bytes 29327360 | tf_op jit(solution)/shard_map/add | solution.py:53
  67.5 0.9 broadcast_multiply_fusion
  69.1 1.2 %slice.249 = bf16[16,16,1,256]{3,0,2,1:T(8,128)(2,1)} slice(f32[16,16,16,256]{3,0,2,1:T(8,128)S(1)} %get-tuple-element.32), slice={[0:16], [0:16], [0:1], [0:256]} | slice | bytes 262144 | tf_op jit(solution)/shard_map/slice | solution.py:38
  70.3 1.6 %collective-permute-start.2 = (bf16[16,16,1,256]{3,0,2,1:T(8,128)(2,1)}, bf16[16,16,1,256]{3,0,2,1:T(8,128)(2,1)}, u32[]{:S(2)}, u32[]{:S(2)}) collective-permute-start(bf16[16,16,1,256]{3,0,2,1:T(8,128)(2,1)} %slice.249), channel_id=1, source_target_pairs={{4,0},{8,4},{12,8},{16,12},{20,16},{24,20},{28,24},{32,28},{36,32}... | collective-permute-start | bytes 393224 | tf_op jit(solution)/shard_map/ppermute | solution.py:20
  71.9 1.8 %slice_multiply_fusion.1 = (f32[16,16,16,255]{3,0,2,1:T(8,128)S(1)}, f32[16,16,16,255]{3,0,2,1:T(8,128)S(1)}) fusion(f32[16,16,16,256]{3,0,2,1:T(8,128)S(1)} %get-tuple-element.54, f32[16,16,255]{2,1,0:T(8,128)S(1)} %copy-done.3, f32[16,16,255]{2,1,0:T(8,128)S(1)} %bitcast.52), kind=kLoop, calls=%fused_computation.1 | loop fusion | flops 2088960 | bytes 17233920 | tf_op jit(solution)/shard_map/mul | solution.py:26
  73.7 3.6 %fusion.8 = f32[16,15,16,256]{3,0,2,1:T(8,128)} fusion(f32[16,16,16,256]{3,0,2,1:T(8,128)S(1)} %get-tuple-element.54, f32[15,16,256]{2,1,0:T(8,128)} %slice_bitcast_fusion), kind=kLoop, calls=%fused_computation.15 | loop fusion | flops 1966080 | bytes 12042240 | tf_op jit(solution)/shard_map/mul | solution.py:47
  77.4 2.3 %slice.200 = f32[16,16,15,256]{3,0,2,1:T(8,128)} slice(f32[16,16,16,256]{3,0,2,1:T(8,128)S(1)} %copy-done.2), slice={[0:16], [0:16], [0:15], [0:256]} | slice | bytes 7864320 | tf_op jit(solution)/shard_map/slice | solution.py:41
  79.7 2.3 %slice.197 = f32[16,16,15,256]{3,0,2,1:T(8,128)} slice(f32[16,16,16,256]{3,0,2,1:T(8,128)S(1)} %get-tuple-element.32), slice={[0:16], [0:16], [1:16], [0:256]} | slice | bytes 7864320 | tf_op jit(solution)/shard_map/slice | solution.py:40
  82.9 0.9 convert_element_type.59
  83.9 8.9 %fusion.7 = f32[16,16,16,256]{3,0,2,1:T(8,128)S(1)} fusion(f32[16,16,1,256]{3,0,2,1:T(8,128)S(1)} %convert_element_type.58, f32[16,16,15,256]{3,0,2,1:T(8,128)} %slice.197, f32[16,16,15,256]{3,0,2,1:T(8,128)} %slice.200, f32[16,16,1,256]{3,0,2,1:T(8,128)S(1)} %convert_element_type.59, f32[16,15,16,256]{3,0,2,1:T(8,128)} %fusion.8, ...), kind=kLoop, calls=%fused_computation.13 | loop fusion | flops 9437184 | bytes 29327360 | tf_op jit(solution)/shard_map/add | solution.py:53
  92.8 4.4 %copy.22 = f32[16,16,16,256]{3,2,1,0:T(8,128)} copy(f32[16,16,16,256]{3,0,2,1:T(8,128)S(1)} %fusion.26) | data formatting | bytes 8388608 | tf_op jit(solution)/shard_map/scatter-add | solution.py:54
  (33 shorter events, 6.5 us)
Async XLA Ops:
  22.5 30.7 %collective-permute-start.1 = (bf16[16,16,1,256]{3,0,2,1:T(8,128)(2,1)}, bf16[16,16,1,256]{3,0,2,1:T(8,128)(2,1)}, u32[]{:S(2)}, u32[]{:S(2)}) collective-permute-start(bf16[16,16,1,256]{3,0,2,1:T(8,128)(2,1)} %slice.250), channel_id=1, source_target_pairs={{252,0},{0,4},{4,8},{8,12},{12,16},{16,20},{20,24},{24,28},{28,32}... | collective-permute-start | bytes 393224 | tf_op jit(solution)/shard_map/ppermute | solution.py:20
  23.4 30.7 %collective-permute-start = (bf16[16,16,1,256]{3,0,2,1:T(8,128)(2,1)}, bf16[16,16,1,256]{3,0,2,1:T(8,128)(2,1)}, u32[]{:S(2)}, u32[]{:S(2)}) collective-permute-start(bf16[16,16,1,256]{3,0,2,1:T(8,128)(2,1)} %slice.251), channel_id=1, source_target_pairs={{4,0},{8,4},{12,8},{16,12},{20,16},{24,20},{28,24},{32,28},{36,32}... | collective-permute-start | bytes 393224 | tf_op jit(solution)/shard_map/ppermute | solution.py:20
  48.6 6.5 %copy-start = (f32[16,16,16,256]{3,2,1,0:T(8,128)S(1)}, f32[16,16,16,256]{3,2,1,0:T(8,128)}, u32[]{:S(2)}) copy-start(f32[16,16,16,256]{3,2,1,0:T(8,128)} %param.9) | copy-start | bytes 12582916
  55.1 12.0 %copy-start.6 = (bf16[64,16,256]{2,1,0:T(8,128)(2,1)S(1)}, bf16[64,16,256]{2,1,0:T(8,128)(2,1)}, u32[]{:S(2)}) copy-start(bf16[64,16,256]{2,1,0:T(8,128)(2,1)} %param.11) | copy-start | bytes 1572868
  55.1 12.0 %copy-start.7 = (s32[16]{0:T(128)S(1)}, s32[16]{0:T(128)}, u32[]{:S(2)}) copy-start(s32[16]{0:T(128)} %param.12) | copy-start | bytes 196
  55.1 12.3 %copy-start.4 = (f32[16,16,256]{2,1,0:T(8,128)S(1)}, f32[16,16,256]{2,1,0:T(8,128)}, u32[]{:S(2)}) copy-start(f32[16,16,256]{2,1,0:T(8,128)} %get-tuple-element.41) | copy-start | bytes 786436
  55.2 12.3 %copy-start.5 = (f32[16,16,256]{2,1,0:T(8,128)S(1)}, f32[16,16,256]{2,1,0:T(8,128)}, u32[]{:S(2)}) copy-start(f32[16,16,256]{2,1,0:T(8,128)} %get-tuple-element.44) | copy-start | bytes 786436
  67.5 4.5 %copy-start.3 = (f32[16,16,255]{2,1,0:T(8,128)S(1)}, f32[16,16,255]{2,1,0:T(8,128)}, u32[]{:S(2)}) copy-start(f32[16,16,255]{2,1,0:T(8,128)} %slice.202) | copy-start | bytes 783364
  68.4 3.5 %copy-start.1 = (f32[16,16,16,256]{3,0,2,1:T(8,128)}, f32[16,16,16,256]{3,0,2,1:T(8,128)S(1)}, u32[]{:S(2)}) copy-start(f32[16,16,16,256]{3,0,2,1:T(8,128)S(1)} %get-tuple-element.31) | copy-start | bytes 12582916
  70.3 11.7 %collective-permute-start.2 = (bf16[16,16,1,256]{3,0,2,1:T(8,128)(2,1)}, bf16[16,16,1,256]{3,0,2,1:T(8,128)(2,1)}, u32[]{:S(2)}, u32[]{:S(2)}) collective-permute-start(bf16[16,16,1,256]{3,0,2,1:T(8,128)(2,1)} %slice.249), channel_id=1, source_target_pairs={{4,0},{8,4},{12,8},{16,12},{20,16},{24,20},{28,24},{32,28},{36,32}... | collective-permute-start | bytes 393224 | tf_op jit(solution)/shard_map/ppermute | solution.py:20
  71.9 11.0 %collective-permute-start.3 = (bf16[16,16,1,256]{3,0,2,1:T(8,128)(2,1)}, bf16[16,16,1,256]{3,0,2,1:T(8,128)(2,1)}, u32[]{:S(2)}, u32[]{:S(2)}) collective-permute-start(bf16[16,16,1,256]{3,0,2,1:T(8,128)(2,1)} %slice.248), channel_id=1, source_target_pairs={{252,0},{0,4},{4,8},{8,12},{12,16},{16,20},{20,24},{24,28},{28,32}... | collective-permute-start | bytes 393224 | tf_op jit(solution)/shard_map/ppermute | solution.py:20
  73.7 3.6 %copy-start.2 = (f32[16,16,16,256]{3,0,2,1:T(8,128)S(1)}, f32[16,16,16,256]{3,0,2,1:T(8,128)}, u32[]{:S(2)}) copy-start(f32[16,16,16,256]{3,0,2,1:T(8,128)} %copy-done.1) | copy-start | bytes 12582916
where the time goes:
time: 97.6 us; the launch traced here: 97.3 us
  other arithmetic  44.2 us (45%)
  local copies, waits for them, and re-layouts  22.7 us (23%)
  blocking collectives  15.9 us (16%)
  starting transfers between devices  10.4 us (11%)
  between operations  3.85 us (4%)
    add x2, other arithmetic, finish(): state = flat + vertical(lam, mixing)  20.8 us
    all_gather x2, blocking collectives, per_device(): metnow = lax.all_gather(locals_list[step], 'rcpt', axis=1, tiled=True)  15.9 us
    ppermute x4, starting transfers between devices, passed_along(): return lax.ppermute(block, axis, route)  10.4 us
    unnamed x1, other arithmetic  6.53 us
    mul x2, other arithmetic, vertical(): flux = coeff[:-1] * (lam[:, 1:] - lam[:, :-1])  6.15 us
    mul x2, other arithmetic, interior(): py = lam * jnp.maximum(cy, 0.0)  4.77 us
    slice x2, local copies, waits for them, and re-layouts, horizontal_shift(): east = jnp.concatenate([px[:, :, 1:], east_edge], axis=2)  4.69 us
    slice x2, local copies, waits for them, and re-layouts, horizontal_shift(): west = jnp.concatenate([west_edge, mx[:, :, :-1]], axis=2)  4.56 us
  transfers between devices with their start and end apart: 4, of which 0 were waited for; matrix products, arithmetic and copies ran while one was open for 28% of the time, Pallas kernels for 0%

commit v1 on v0

--- a/solution.py
+++ b/solution.py
@@ -1,9 +1,26 @@
+import functools
 import jax
 import jax.numpy as jnp
 from jax import lax
 from jax.sharding import PartitionSpec as P
 
 STEPS = 2
+
+
+def cover_chains(array_in, in_dim):
+    current_arr = jnp.concatenate(
+        lax.all_to_all(
+            jnp.stack([array_in for _ in range(lax.axis_size("rcpt"))], 0),
+            "rcpt",
+            concat_axis=0,
+            split_axis=0,
+        ),
+        in_dim,
+    )
+    return current_arr
+
+
+_group_copies = functools.partial(cover_chains, in_dim=1)
 
 
 def for_sending(x):
@@ -67,7 +84,7 @@
         for step in range(STEPS)
     ]
     for step in range(STEPS):
-        metnow = lax.all_gather(locals_list[step], "rcpt", axis=1, tiled=True)
+        metnow = _group_copies(locals_list[step])
         lam_next = finish(lam, horizontal_shift(lam, metnow), metnow[2], source_rows)
         lam = lam_next
     return lam

time: 97.6 us -> 102 us (1.045)
  starting transfers between devices: 10.4 us -> 14.7 us
  blocking collectives: 15.9 us -> 12 us
  other arithmetic: 44.2 us -> 46.6 us
  local copies, waits for them, and re-layouts: 22.7 us -> 24.2 us
    all_gather x2 -> x0, blocking collectives: 15.9 us -> none  [per_device(): metnow = lax.all_gather(locals_list[step], 'rcpt', axis=1, tiled=True)]
    all_to_all x0 -> x1, blocking collectives: none -> 12 us  [cover_chains(): lax.all_to_all(jnp.stack([array_in for _ in range(lax.axis_size('rcpt'))]...]
    all_to_all x0 -> x1, starting transfers between devices: none -> 4.47 us  [cover_chains(): lax.all_to_all(jnp.stack([array_in for _ in range(lax.axis_size('rcpt'))]...]
    slice x2, local copies, waits for them, and re-layouts: 4.69 us -> 7.08 us  [horizontal_shift(): east = jnp.concatenate([px[:, :, 1:], east_edge], axis=2)]
    mul x2, other arithmetic: 4.77 us -> 6.76 us  [interior(): py = lam * jnp.maximum(cy, 0.0)]
    slice x2, local copies, waits for them, and re-layouts: 1.73 us -> 0.25 us  [interior(): north = jnp.concatenate([py[..., 1:], zero], axis=3)]
    mul x2 -> x0, other arithmetic: 1.17 us -> none  [interior(): return lam * (1.0 - jnp.abs(cx) - jnp.abs(cy)) + east - west + north - south]
  transfers between devices with their start and end apart: 4 -> 5, of which waited for: 0 -> 0; matrix products, arithmetic and copies ran while one was open for 28% -> 36% of each run, Pallas kernels for 0% -> 0%
where the time goes in v1:
time: 102 us
  other arithmetic  46.6 us (46%)
  local copies, waits for them, and re-layouts  24.2 us (24%)
  starting transfers between devices  14.7 us (14%)
  blocking collectives  12 us (12%)
  between operations  4.07 us (4%)
    add x2, other arithmetic, finish(): state = flat + vertical(lam, mixing)  21.3 us
    all_to_all x1, blocking collectives, cover_chains(): lax.all_to_all(jnp.stack([array_in for _ in range(lax.axis_size('rcpt'))]...  12 us
    ppermute x4, starting transfers between devices, passed_along(): return lax.ppermute(block, axis, route)  10.2 us
    slice x2, local copies, waits for them, and re-layouts, horizontal_shift(): east = jnp.concatenate([px[:, :, 1:], east_edge], axis=2)  7.08 us
    mul x2, other arithmetic, interior(): py = lam * jnp.maximum(cy, 0.0)  6.76 us
    unnamed x1, other arithmetic  6.53 us
    mul x2, other arithmetic, vertical(): flux = coeff[:-1] * (lam[:, 1:] - lam[:, :-1])  6.15 us
    slice x2, local copies, waits for them, and re-layouts, horizontal_shift(): west = jnp.concatenate([west_edge, mx[:, :, :-1]], axis=2)  4.72 us
  transfers between devices with their start and end apart: 5, of which 0 were waited for; matrix products, arithmetic and copies ran while one was open for 36% of the time, Pallas kernels for 0%

profile of v1, /device:TPU:1, one launch (start us, length us, event | category | flops | bytes accessed | tf_op | source)
XLA Modules:
  0.0 101.8 jit_solution(1009813860522566629)
XLA Ops:
  0.0 1.3 %fusion.22 = (s32[1]{0:T(128)}, s32[1]{0:T(128)}) fusion(s32[2]{0:T(128)} %param.13), kind=kLoop, calls=%fused_computation.57 | loop fusion | bytes 16 | tf_op jit(solution)/shard_map/slice | solution.py:83
  5.1 1.0 dynamic-slice_bitcast_fusion
  6.1 12.0 %all_to_all.10 = bf16[4,3,4,16,256]{4,3,2,1,0:T(8,128)(2,1)S(1)} all-to-all(bf16[4,3,4,16,256]{4,3,2,1,0:T(8,128)(2,1)S(1)} %stack.4), channel_id=1, replica_groups=mesh['tile'=64,'rcpt'=4] {'rcpt'}, dimensions={0} | all-to-all | bytes 786432 | tf_op jit(solution)/shard_map/all_to_all | solution.py:12
  18.9 4.5 %all-to-all-start.1 = ((bf16[4,3,4,16,256]{4,3,2,1,0:T(8,128)(2,1)}), bf16[4,3,4,16,256]{4,3,2,1,0:T(8,128)(2,1)S(1)}, u32[]{:S(2)}, u32[]{:S(2)}) async-start(bf16[4,3,4,16,256]{4,3,2,1,0:T(8,128)(2,1)} %stack.5), calls=%async_computation.1 | async-start | bytes 786432 | tf_op jit(solution)/shard_map/all_to_all | solution.py:12
  23.7 6.5 %fusion.21 = (f32[16,16,16,256]{3,0,2,1:T(8,128)S(1)}, f32[16,16,16,256]{3,0,2,1:T(8,128)S(1)}, f32[16,16,16,256]{3,0,2,1:T(8,128)S(1)}) fusion(f32[16,16,16,256]{3,2,1,0:T(8,128)} %param.9, f32[16,16,256]{2,1,0:T(8,128)S(1)} %bitcast.48, f32[16,16,256]{2,1,0:T(8,128)S(1)} %bitcast.49), kind=kLoop, calls=%fused_computation.56 | loop fusion | flops 2097152 | bytes 17301504 | tf_op args[0]
  31.0 1.2 %slice.240 = bf16[16,16,1,256]{3,0,2,1:T(8,128)(2,1)} slice(f32[16,16,16,256]{3,0,2,1:T(8,128)S(1)} %get-tuple-element.37), slice={[0:16], [0:16], [15:16], [0:256]} | slice | bytes 262144 | tf_op jit(solution)/shard_map/slice | solution.py:56
  32.3 8.7 %collective-permute-start = (bf16[16,16,1,256]{3,0,2,1:T(8,128)(2,1)}, bf16[16,16,1,256]{3,0,2,1:T(8,128)(2,1)}, u32[]{:S(2)}, u32[]{:S(2)}) collective-permute-start(bf16[16,16,1,256]{3,0,2,1:T(8,128)(2,1)} %slice.241), channel_id=1, source_target_pairs={{4,0},{8,4},{12,8},{16,12},{20,16},{24,20},{28,24},{32,28},{36,32}... | collective-permute-start | bytes 393224 | tf_op jit(solution)/shard_map/ppermute | solution.py:37
  41.0 5.0 %slice_multiply_fusion.3 = (f32[16,16,16,255]{3,0,2,1:T(8,128)}, f32[16,16,16,255]{3,0,2,1:T(8,128)}) fusion(f32[16,16,16,256]{3,0,2,1:T(8,128)S(1)} %get-tuple-element.35, f32[16,16,255]{2,1,0:T(8,128)S(1)} %slice.179, f32[16,16,255]{2,1,0:T(8,128)S(1)} %bitcast.47), kind=kLoop, calls=%fused_computation.3 | loop fusion | flops 2088960 | bytes 17233920 | tf_op jit(solution)/shard_map/mul | solution.py:43
  46.0 2.5 %fusion.9 = f32[16,15,16,256]{3,0,2,1:T(8,128)} fusion(f32[16,16,16,256]{3,0,2,1:T(8,128)S(1)} %get-tuple-element.35, f32[15,16,256]{2,1,0:T(8,128)S(1)} %slice.183), kind=kLoop, calls=%fused_computation.17 | loop fusion | flops 1966080 | bytes 12042240 | tf_op jit(solution)/shard_map/mul | solution.py:64
  48.7 4.7 %slice.174 = f32[16,16,15,256]{3,0,2,1:T(8,128)} slice(f32[16,16,16,256]{3,0,2,1:T(8,128)} %copy-done.7), slice={[0:16], [0:16], [1:16], [0:256]} | slice | bytes 7864320 | tf_op jit(solution)/shard_map/slice | solution.py:57
  53.4 2.4 %slice.177 = f32[16,16,15,256]{3,0,2,1:T(8,128)} slice(f32[16,16,16,256]{3,0,2,1:T(8,128)S(1)} %copy-done.6), slice={[0:16], [0:16], [0:15], [0:256]} | slice | bytes 7864320 | tf_op jit(solution)/shard_map/slice | solution.py:58
  56.7 1.7 %convert_element_type.86 = f32[16,16,1,256]{3,0,2,1:T(8,128)S(1)} convert(bf16[16,16,1,256]{3,0,2,1:T(8,128)(2,1)} %collective-permute-done.1) | non-fusion elementwise | flops 65536 | bytes 393216 | tf_op jit(solution)/shard_map/convert_element_type | solution.py:58
  58.4 0.9 convert_element_type.85
  59.3 12.3 %fusion.3 = f32[16,16,16,256]{3,0,2,1:T(8,128)S(1)} fusion(f32[16,16,1,256]{3,0,2,1:T(8,128)S(1)} %convert_element_type.85, f32[16,16,15,256]{3,0,2,1:T(8,128)} %slice.174, f32[16,16,15,256]{3,0,2,1:T(8,128)} %slice.177, f32[16,16,1,256]{3,0,2,1:T(8,128)S(1)} %convert_element_type.86, f32[16,15,16,256]{3,0,2,1:T(8,128)} %fusion.9, ...), kind=kLoop, calls=%fused_computation.8 | loop fusion | flops 9437184 | bytes 29327360 | tf_op jit(solution)/shard_map/add | solution.py:70
  72.0 0.9 broadcast_multiply_fusion
  73.7 1.2 %slice.239 = bf16[16,16,1,256]{3,0,2,1:T(8,128)(2,1)} slice(f32[16,16,16,256]{3,0,2,1:T(8,128)S(1)} %get-tuple-element.32), slice={[0:16], [0:16], [0:1], [0:256]} | slice | bytes 262144 | tf_op jit(solution)/shard_map/slice | solution.py:55
  74.8 1.5 %collective-permute-start.2 = (bf16[16,16,1,256]{3,0,2,1:T(8,128)(2,1)}, bf16[16,16,1,256]{3,0,2,1:T(8,128)(2,1)}, u32[]{:S(2)}, u32[]{:S(2)}) collective-permute-start(bf16[16,16,1,256]{3,0,2,1:T(8,128)(2,1)} %slice.239), channel_id=1, source_target_pairs={{4,0},{8,4},{12,8},{16,12},{20,16},{24,20},{28,24},{32,28},{36,32}... | collective-permute-start | bytes 393224 | tf_op jit(solution)/shard_map/ppermute | solution.py:37
  76.3 1.8 %slice_multiply_fusion.1 = (f32[16,16,16,255]{3,0,2,1:T(8,128)S(1)}, f32[16,16,16,255]{3,0,2,1:T(8,128)S(1)}) fusion(f32[16,16,16,256]{3,0,2,1:T(8,128)S(1)} %get-tuple-element.54, f32[16,16,255]{2,1,0:T(8,128)S(1)} %slice.194, f32[16,16,255]{2,1,0:T(8,128)S(1)} %bitcast.46), kind=kLoop, calls=%fused_computation.1 | loop fusion | flops 2088960 | bytes 17233920 | tf_op jit(solution)/shard_map/mul | solution.py:43
  78.1 3.6 %fusion.8 = f32[16,15,16,256]{3,0,2,1:T(8,128)} fusion(f32[16,16,16,256]{3,0,2,1:T(8,128)S(1)} %get-tuple-element.54, f32[15,16,256]{2,1,0:T(8,128)} %slice.198), kind=kLoop, calls=%fused_computation.15 | loop fusion | flops 1966080 | bytes 12042240 | tf_op jit(solution)/shard_map/mul | solution.py:64
  81.8 2.3 %slice.192 = f32[16,16,15,256]{3,0,2,1:T(8,128)} slice(f32[16,16,16,256]{3,0,2,1:T(8,128)S(1)} %copy-done.4), slice={[0:16], [0:16], [0:15], [0:256]} | slice | bytes 7864320 | tf_op jit(solution)/shard_map/slice | solution.py:58
  84.0 2.3 %slice.189 = f32[16,16,15,256]{3,0,2,1:T(8,128)} slice(f32[16,16,16,256]{3,0,2,1:T(8,128)S(1)} %get-tuple-element.32), slice={[0:16], [0:16], [1:16], [0:256]} | slice | bytes 7864320 | tf_op jit(solution)/shard_map/slice | solution.py:57
  87.3 0.9 convert_element_type.91
  88.3 9.0 %fusion.7 = f32[16,16,16,256]{3,0,2,1:T(8,128)S(1)} fusion(f32[16,16,1,256]{3,0,2,1:T(8,128)S(1)} %convert_element_type.90, f32[16,16,15,256]{3,0,2,1:T(8,128)} %slice.189, f32[16,16,15,256]{3,0,2,1:T(8,128)} %slice.192, f32[16,16,1,256]{3,0,2,1:T(8,128)S(1)} %convert_element_type.91, f32[16,15,16,256]{3,0,2,1:T(8,128)} %fusion.8, ...), kind=kLoop, calls=%fused_computation.13 | loop fusion | flops 9437184 | bytes 29327360 | tf_op jit(solution)/shard_map/add | solution.py:70
  97.4 4.4 %copy.31 = f32[16,16,16,256]{3,2,1,0:T(8,128)} copy(f32[16,16,16,256]{3,0,2,1:T(8,128)S(1)} %fusion.16) | data formatting | bytes 8388608 | tf_op jit(solution)/shard_map/scatter-add | solution.py:71
  (40 shorter events, 5.1 us)
Async XLA Ops:
  18.9 29.6 %all-to-all-start.1 = ((bf16[4,3,4,16,256]{4,3,2,1,0:T(8,128)(2,1)}), bf16[4,3,4,16,256]{4,3,2,1,0:T(8,128)(2,1)S(1)}, u32[]{:S(2)}, u32[]{:S(2)}) async-start(bf16[4,3,4,16,256]{4,3,2,1,0:T(8,128)(2,1)} %stack.5), calls=%async_computation.1 | async-start | bytes 786432 | tf_op jit(solution)/shard_map/all_to_all | solution.py:12
  30.3 15.7 %copy-start.5 = (f32[16,16,16,256]{3,0,2,1:T(8,128)}, f32[16,16,16,256]{3,0,2,1:T(8,128)S(1)}, u32[]{:S(2)}) copy-start(f32[16,16,16,256]{3,0,2,1:T(8,128)S(1)} %get-tuple-element.37) | copy-start | bytes 12582916
  30.3 15.7 %copy-start.7 = (f32[16,16,16,256]{3,0,2,1:T(8,128)}, f32[16,16,16,256]{3,0,2,1:T(8,128)S(1)}, u32[]{:S(2)}) copy-start(f32[16,16,16,256]{3,0,2,1:T(8,128)S(1)} %get-tuple-element.36) | copy-start | bytes 12582916
  32.2 24.5 %collective-permute-start.1 = (bf16[16,16,1,256]{3,0,2,1:T(8,128)(2,1)}, bf16[16,16,1,256]{3,0,2,1:T(8,128)(2,1)}, u32[]{:S(2)}, u32[]{:S(2)}) collective-permute-start(bf16[16,16,1,256]{3,0,2,1:T(8,128)(2,1)} %slice.240), channel_id=1, source_target_pairs={{252,0},{0,4},{4,8},{8,12},{12,16},{16,20},{20,24},{24,28},{28,32}... | collective-permute-start | bytes 393224 | tf_op jit(solution)/shard_map/ppermute | solution.py:37
  32.3 26.1 %collective-permute-start = (bf16[16,16,1,256]{3,0,2,1:T(8,128)(2,1)}, bf16[16,16,1,256]{3,0,2,1:T(8,128)(2,1)}, u32[]{:S(2)}, u32[]{:S(2)}) collective-permute-start(bf16[16,16,1,256]{3,0,2,1:T(8,128)(2,1)} %slice.241), channel_id=1, source_target_pairs={{4,0},{8,4},{12,8},{16,12},{20,16},{24,20},{28,24},{32,28},{36,32}... | collective-permute-start | bytes 393224 | tf_op jit(solution)/shard_map/ppermute | solution.py:37
  48.5 4.9 %copy-start.6 = (f32[16,16,16,256]{3,0,2,1:T(8,128)S(1)}, f32[16,16,16,256]{3,0,2,1:T(8,128)}, u32[]{:S(2)}) copy-start(f32[16,16,16,256]{3,0,2,1:T(8,128)} %copy-done.5) | copy-start | bytes 12582916
  48.6 10.7 %copy-start.2 = (f32[16,16,16,255]{3,0,2,1:T(8,128)S(1)}, f32[16,16,16,255]{3,0,2,1:T(8,128)}, u32[]{:S(2)}) copy-start(f32[16,16,16,255]{3,0,2,1:T(8,128)} %get-tuple-element.34) | copy-start | bytes 12533764
  53.4 5.9 %copy-start = (f32[16,16,16,256]{3,2,1,0:T(8,128)S(1)}, f32[16,16,16,256]{3,2,1,0:T(8,128)}, u32[]{:S(2)}) copy-start(f32[16,16,16,256]{3,2,1,0:T(8,128)} %param.9) | copy-start | bytes 12582916
  53.4 5.9 %copy-start.1 = (f32[16,16,16,255]{3,0,2,1:T(8,128)S(1)}, f32[16,16,16,255]{3,0,2,1:T(8,128)}, u32[]{:S(2)}) copy-start(f32[16,16,16,255]{3,0,2,1:T(8,128)} %get-tuple-element.33) | copy-start | bytes 12533764
  59.3 12.3 %copy-start.8 = (bf16[64,16,256]{2,1,0:T(8,128)(2,1)S(1)}, bf16[64,16,256]{2,1,0:T(8,128)(2,1)}, u32[]{:S(2)}) copy-start(bf16[64,16,256]{2,1,0:T(8,128)(2,1)} %param.11) | copy-start | bytes 1572868
  59.3 12.3 %copy-start.9 = (s32[16]{0:T(128)S(1)}, s32[16]{0:T(128)}, u32[]{:S(2)}) copy-start(s32[16]{0:T(128)} %param.12) | copy-start | bytes 196
  72.9 3.4 %copy-start.3 = (f32[16,16,16,256]{3,0,2,1:T(8,128)}, f32[16,16,16,256]{3,0,2,1:T(8,128)S(1)}, u32[]{:S(2)}) copy-start(f32[16,16,16,256]{3,0,2,1:T(8,128)S(1)} %get-tuple-element.31) | copy-start | bytes 12582916
  74.8 11.6 %collective-permute-start.2 = (bf16[16,16,1,256]{3,0,2,1:T(8,128)(2,1)}, bf16[16,16,1,256]{3,0,2,1:T(8,128)(2,1)}, u32[]{:S(2)}, u32[]{:S(2)}) collective-permute-start(bf16[16,16,1,256]{3,0,2,1:T(8,128)(2,1)} %slice.239), channel_id=1, source_target_pairs={{4,0},{8,4},{12,8},{16,12},{20,16},{24,20},{28,24},{32,28},{36,32}... | collective-permute-start | bytes 393224 | tf_op jit(solution)/shard_map/ppermute | solution.py:37
  76.3 11.0 %collective-permute-start.3 = (bf16[16,16,1,256]{3,0,2,1:T(8,128)(2,1)}, bf16[16,16,1,256]{3,0,2,1:T(8,128)(2,1)}, u32[]{:S(2)}, u32[]{:S(2)}) collective-permute-start(bf16[16,16,1,256]{3,0,2,1:T(8,128)(2,1)} %slice.238), channel_id=1, source_target_pairs={{252,0},{0,4},{4,8},{8,12},{12,16},{16,20},{20,24},{24,28},{28,32}... | collective-permute-start | bytes 393224 | tf_op jit(solution)/shard_map/ppermute | solution.py:37
  78.1 3.6 %copy-start.4 = (f32[16,16,16,256]{3,0,2,1:T(8,128)S(1)}, f32[16,16,16,256]{3,0,2,1:T(8,128)}, u32[]{:S(2)}) copy-start(f32[16,16,16,256]{3,0,2,1:T(8,128)} %copy-done.3) | copy-start | bytes 12582916
